TPU v7x, 32 devices: a whole 2x2x4 slice. The times are simulated.
32 devices in a mesh: win: 2 (over x), sub: 16 (over z, y, core).
Axes of the slice: x: 2, y: 2, z: 4, core: 2. Of those that a mesh axis runs over, the one named last changes fastest.
Arguments:
- pulses: bfloat16 [32, 80, 2, 4096], P(('win', 'sub')), parts along dimension 0, may hold values from -6 to 6
- offsets: int32 [32, 80], P(('win', 'sub')), parts along dimension 0, may hold values from 0 to 3968
- geometry: float32 [32, 3, 80], P(('win', 'sub')), parts along dimension 0, may hold values from -1 to 1
- counts: int32 [32], P(('win', 'sub')), parts along dimension 0, may hold values from 48 to 80, as said below
Outputs:
- frames: float32 [32, 2, 32, 512], P(('win', 'sub')), parts along dimension 0
- cumulative: float32 [32, 2, 32, 512], P(('win', 'sub')), parts along dimension 0
There are 2 independent parts, one for each index of `win`. A program takes and returns all parts, laid end to end along the dimension named above; each array names one. Nothing has to cross between parts.
Inputs may be any that keep to these rules, and one draw needn't show every extreme that they name: Subaperture s holds its pulses in slots 0 to counts[s] - 1; the other slots are unused. Some subaperture has 80 pulses and some 48.
All inputs are finite; a program needn't handle non-finite values.
Results may differ from a plain program's by a relative error of at most 0.004.
Values sent between devices are 32-bit elements; how exact they have to be, the bound alone decides.
A program may use at most 192 MiB of HBM per device.

v0:
```python
import math
import jax
import jax.numpy as jnp
from jax import lax
from jax.sharding import PartitionSpec as P

ROWS = 32
COLS = 512
BINS = 128


def spectrum_of(pulse_rows, vertical_offset_along, geometry_sub, count, width):
    slots = pulse_rows.shape[0]
    windows = jax.vmap(lambda one_row, offset: lax.dynamic_slice_in_dim(one_row, offset, width, 1))(
        pulse_rows, vertical_offset_along
    ).astype(jnp.float32)
    index = jnp.arange(width, dtype=jnp.int32)
    shifted = index - width // 2
    turns = index[:, None] * shifted[None, :] % width
    angle = 2.0 * math.pi / width * turns.astype(jnp.float32)
    cosine = jnp.cos(angle)
    sine = jnp.sin(angle)
    highest = lax.Precision.HIGHEST
    real_in = windows[:, 0]
    imag_in = windows[:, 1]
    real_out = (
        jnp.dot(real_in, cosine, precision=highest) + jnp.dot(imag_in, sine, precision=highest)
    ) / width
    imag_out = (
        jnp.dot(imag_in, cosine, precision=highest) - jnp.dot(real_in, sine, precision=highest)
    ) / width
    viewing_bearing = 2.0 * math.pi * (shifted.astype(jnp.float32) / width + 0.37)
    scene_middle = width / 2.0 + width / 16.0 * geometry_sub[0]
    radar_frequency = 2.0 * math.pi / 100.0 * (37 * vertical_offset_along % 100).astype(jnp.float32)
    signal_argument = viewing_bearing[None, :] * scene_middle[:, None] + radar_frequency[:, None]
    live = (jnp.arange(slots, dtype=jnp.int32) < count).astype(jnp.float32) / math.sqrt(slots)
    cos_phase = jnp.cos(signal_argument)
    sin_phase = jnp.sin(signal_argument)
    coefficient_real = live[:, None] * (real_out * cos_phase - imag_out * sin_phase)
    coef_im = live[:, None] * (real_out * sin_phase + imag_out * cos_phase)
    return (coefficient_real, coef_im, viewing_bearing)


def block_product(
    coefficient_real, coef_im, viewing_bearing, row_slope, column_gradient, rows, cols
):
    xpos = (jnp.arange(rows, dtype=jnp.int32) - rows // 2).astype(jnp.float32)
    ypos = (jnp.arange(cols, dtype=jnp.int32) - cols // 2).astype(jnp.float32)
    angle_x = xpos[:, None, None] * (viewing_bearing[None, :] * row_slope[:, None])[None]
    cosine_x = jnp.cos(angle_x)
    sine_x = jnp.sin(angle_x)
    left_re = coefficient_real[None] * cosine_x - coef_im[None] * sine_x
    left_im = coefficient_real[None] * sine_x + coef_im[None] * cosine_x
    left = jnp.concatenate([left_re.reshape(rows, -1), left_im.reshape(rows, -1)], axis=1).astype(
        jnp.bfloat16
    )
    angle_y = (viewing_bearing[None, :] * column_gradient[:, None])[:, :, None] * ypos[
        None, None, :
    ]
    right_re = jnp.cos(angle_y).reshape(-1, cols)
    right_im = jnp.sin(angle_y).reshape(-1, cols)
    upper = jnp.concatenate([right_re, right_im], axis=1)
    lower = jnp.concatenate([-right_im, right_re], axis=1)
    right = jnp.concatenate([upper, lower], axis=0).astype(jnp.bfloat16)
    return jnp.dot(left, right, preferred_element_type=jnp.float32)


def shards(pulses, offsets, geometry, counts):
    rows = ROWS
    cols = COLS
    width = BINS
    slots = pulses.shape[1]
    count = counts[0]
    geometry_sub = geometry[0]
    coefficient_real, coef_im, viewing_bearing = spectrum_of(
        pulses[0], offsets[0], geometry_sub, count, width
    )
    row_slope = 0.05 * geometry_sub[1]
    column_gradient = 0.05 * geometry_sub[2]

    def add_block(step, total):
        start = (step * 8).astype(jnp.int32)
        part_re = lax.dynamic_slice_in_dim(coefficient_real, start, 8, 0)
        part_im = lax.dynamic_slice_in_dim(coef_im, start, 8, 0)
        slope_r = lax.dynamic_slice_in_dim(row_slope, start, 8, 0)
        slope_c = lax.dynamic_slice_in_dim(column_gradient, start, 8, 0)
        return total + block_product(
            part_re, part_im, viewing_bearing, slope_r, slope_c, rows, cols
        )

    empty = jnp.zeros((rows, 2 * cols), jnp.float32)
    total = lax.fori_loop(0, slots // 8, add_block, empty)
    own = jnp.stack([total[:, :cols], total[:, cols:]], axis=0)[None]
    flattened = own.reshape(1, 2 * rows * cols)
    by_pixels = lax.all_to_all(flattened, "sub", split_axis=1, concat_axis=0, tiled=True)
    members = by_pixels.shape[0]
    running = jnp.cumsum(by_pixels, axis=0)
    delayed = jnp.concatenate([jnp.zeros((8, running.shape[1]), jnp.float32), running[:-8]], axis=0)
    frame_rows = (running - delayed) / math.sqrt(8.0)
    magnitude_factor = jnp.sqrt(jnp.arange(1, members + 1, dtype=jnp.int32).astype(jnp.float32))
    cumulative_rows = running / magnitude_factor[:, None]
    frames_back, cumulative_back = (
        lax.all_to_all(frame_rows, "sub", split_axis=0, concat_axis=1, tiled=True),
        lax.all_to_all(cumulative_rows, "sub", split_axis=0, concat_axis=1, tiled=True),
    )
    frames = frames_back.reshape(1, 2, rows, cols)
    cumulative = cumulative_back.reshape(1, 2, rows, cols)
    return (frames, cumulative)


def solution(mesh):
    return jax.shard_map(
        shards,
        mesh=mesh,
        in_specs=(
            P(("win", "sub"), None, None, None),
            P(("win", "sub"), None),
            P(("win", "sub"), None, None),
            P(("win", "sub")),
        ),
        out_specs=(P(("win", "sub"), None, None, None), P(("win", "sub"), None, None, None)),
        check_vma=False,
    )
```

profile of v0, /device:TPU:0, one launch (start us, length us, event | category | flops | bytes accessed | tf_op | source)
XLA Modules:
  0.0 226.5 jit_solution(11494692594200224226)
XLA Ops:
  0.7 56.8 %copy.10 = bf16[1,80,2,4096]{2,1,3,0:T(8,128)(2,1)} copy(bf16[1,80,2,4096]{3,2,1,0:T(2,128)(2,1)} %param.6) | data formatting | bytes 2621440 | tf_op args[0]
  57.5 17.8 %gather_fusion = bf16[80,2,128]{1,0,2:T(8,128)(2,1)S(1)} fusion(bf16[80,2,4096]{1,0,2:T(8,128)(2,1)} %bitcast.1, s32[80]{0:T(128)S(1)} %fusion.56), kind=kCustom, calls=%fused_computation | custom fusion | bytes 82880 | tf_op jit(solution)/shard_map/vmap()/gather | solution.py:14
  75.3 3.2 %fusion.73 = (bf16[80,1,128]{1,0,2:T(8,128)(2,1)}, bf16[80,1,128]{1,0,2:T(8,128)(2,1)}) fusion(bf16[80,2,128]{1,0,2:T(8,128)(2,1)S(1)} %gather_fusion), kind=kLoop, calls=%fused_computation.101 | loop fusion | bytes 81920 | tf_op jit(solution)/shard_map/slice | solution.py:24
  78.4 3.1 %copy.11 = bf16[80,1,128]{2,0,1:T(8,128)(2,1)S(1)} copy(bf16[80,1,128]{1,0,2:T(8,128)(2,1)} %get-tuple-element.243) | data formatting | bytes 40960 | tf_op jit(solution)/shard_map/slice | solution.py:24
  81.5 1.6 copy.12
  83.1 0.4 fusion.43
  83.5 0.4 fusion.41
  84.0 0.4 fusion.30
  85.1 0.4 add_multiply_fusion.1
  85.5 100.0 %while.17 = (s32[]{:T(128)}, f32[32,1024]{1,0:T(8,128)S(1)}, f32[80,128]{1,0:T(8,128)S(1)}, f32[80]{0:T(128)S(1)}, f32[80,128]{1,0:T(8,128)S(1)}, /*index=5*/f32...) while((s32[]{:T(128)}, f32[32,1024]{1,0:T(8,128)S(1)}, ...), condition=%wide.region_1.2_spmd.clone.clone, body=%wide.region_0.1_spmd.clone.clone.sunk | while | flops 154242752 | bytes 6879337 | solution.py:92
  85.8 0.1 dynamic_slice.55
  85.9 0.6 fusion.82
  86.5 0.1 dynamic_slice.54
  86.7 8.2 %fusion.81 = (bf16[1024,512]{1,0:T(8,128)(2,1)S(1)}, bf16[1024,512]{1,0:T(8,128)(2,1)S(1)}, bf16[1024,512]{1,0:T(8,128)(2,1)S(1)}) fusion(f32[512]{0:T(512)S(1)} %add_convert_fusion.4, f32[1024]{0:T(1024)S(1)} %bitcast_multiply_fusion.4), kind=kLoop, calls=%fused_computation.13.clone.1 | loop fusion | flops 2621440 | bytes 3151872 | tf_op jit(solution)/shard_map/convert.5
  94.9 0.8 fusion.83
  95.7 0.1 dynamic_slice.55
  95.9 0.6 fusion.82
  96.6 8.2 %fusion.81 = (bf16[1024,512]{1,0:T(8,128)(2,1)S(1)}, bf16[1024,512]{1,0:T(8,128)(2,1)S(1)}, bf16[1024,512]{1,0:T(8,128)(2,1)S(1)}) fusion(f32[512]{0:T(512)S(1)} %add_convert_fusion.4, f32[1024]{0:T(1024)S(1)} %bitcast_multiply_fusion.4), kind=kLoop, calls=%fused_computation.13.clone.1 | loop fusion | flops 2621440 | bytes 3151872 | tf_op jit(solution)/shard_map/convert.5
  104.9 0.8 fusion.83
  105.9 0.6 fusion.82
  106.5 0.1 dynamic_slice.54
  106.6 8.2 %fusion.81 = (bf16[1024,512]{1,0:T(8,128)(2,1)S(1)}, bf16[1024,512]{1,0:T(8,128)(2,1)S(1)}, bf16[1024,512]{1,0:T(8,128)(2,1)S(1)}) fusion(f32[512]{0:T(512)S(1)} %add_convert_fusion.4, f32[1024]{0:T(1024)S(1)} %bitcast_multiply_fusion.4), kind=kLoop, calls=%fused_computation.13.clone.1 | loop fusion | flops 2621440 | bytes 3151872 | tf_op jit(solution)/shard_map/convert.5
  114.9 0.8 fusion.83
  115.7 0.1 dynamic_slice.55
  115.9 0.6 fusion.82
  116.6 8.2 %fusion.81 = (bf16[1024,512]{1,0:T(8,128)(2,1)S(1)}, bf16[1024,512]{1,0:T(8,128)(2,1)S(1)}, bf16[1024,512]{1,0:T(8,128)(2,1)S(1)}) fusion(f32[512]{0:T(512)S(1)} %add_convert_fusion.4, f32[1024]{0:T(1024)S(1)} %bitcast_multiply_fusion.4), kind=kLoop, calls=%fused_computation.13.clone.1 | loop fusion | flops 2621440 | bytes 3151872 | tf_op jit(solution)/shard_map/convert.5
  124.8 0.8 fusion.83
  125.9 0.6 fusion.82
  126.6 8.2 %fusion.81 = (bf16[1024,512]{1,0:T(8,128)(2,1)S(1)}, bf16[1024,512]{1,0:T(8,128)(2,1)S(1)}, bf16[1024,512]{1,0:T(8,128)(2,1)S(1)}) fusion(f32[512]{0:T(512)S(1)} %add_convert_fusion.4, f32[1024]{0:T(1024)S(1)} %bitcast_multiply_fusion.4), kind=kLoop, calls=%fused_computation.13.clone.1 | loop fusion | flops 2621440 | bytes 3151872 | tf_op jit(solution)/shard_map/convert.5
  134.8 0.8 fusion.83
  135.8 0.6 fusion.82
  136.4 0.1 dynamic_slice.54
  136.6 8.2 %fusion.81 = (bf16[1024,512]{1,0:T(8,128)(2,1)S(1)}, bf16[1024,512]{1,0:T(8,128)(2,1)S(1)}, bf16[1024,512]{1,0:T(8,128)(2,1)S(1)}) fusion(f32[512]{0:T(512)S(1)} %add_convert_fusion.4, f32[1024]{0:T(1024)S(1)} %bitcast_multiply_fusion.4), kind=kLoop, calls=%fused_computation.13.clone.1 | loop fusion | flops 2621440 | bytes 3151872 | tf_op jit(solution)/shard_map/convert.5
  144.8 0.8 fusion.83
  145.6 0.1 dynamic_slice.55
  145.8 0.6 fusion.82
  146.5 8.2 %fusion.81 = (bf16[1024,512]{1,0:T(8,128)(2,1)S(1)}, bf16[1024,512]{1,0:T(8,128)(2,1)S(1)}, bf16[1024,512]{1,0:T(8,128)(2,1)S(1)}) fusion(f32[512]{0:T(512)S(1)} %add_convert_fusion.4, f32[1024]{0:T(1024)S(1)} %bitcast_multiply_fusion.4), kind=kLoop, calls=%fused_computation.13.clone.1 | loop fusion | flops 2621440 | bytes 3151872 | tf_op jit(solution)/shard_map/convert.5
  154.8 0.8 fusion.83
  155.8 0.6 fusion.82
  156.5 8.2 %fusion.81 = (bf16[1024,512]{1,0:T(8,128)(2,1)S(1)}, bf16[1024,512]{1,0:T(8,128)(2,1)S(1)}, bf16[1024,512]{1,0:T(8,128)(2,1)S(1)}) fusion(f32[512]{0:T(512)S(1)} %add_convert_fusion.4, f32[1024]{0:T(1024)S(1)} %bitcast_multiply_fusion.4), kind=kLoop, calls=%fused_computation.13.clone.1 | loop fusion | flops 2621440 | bytes 3151872 | tf_op jit(solution)/shard_map/convert.5
  164.8 0.8 fusion.83
  165.6 0.1 dynamic_slice.55
  165.8 0.6 fusion.82
  166.3 0.1 dynamic_slice.54
  166.5 8.2 %fusion.81 = (bf16[1024,512]{1,0:T(8,128)(2,1)S(1)}, bf16[1024,512]{1,0:T(8,128)(2,1)S(1)}, bf16[1024,512]{1,0:T(8,128)(2,1)S(1)}) fusion(f32[512]{0:T(512)S(1)} %add_convert_fusion.4, f32[1024]{0:T(1024)S(1)} %bitcast_multiply_fusion.4), kind=kLoop, calls=%fused_computation.13.clone.1 | loop fusion | flops 2621440 | bytes 3151872 | tf_op jit(solution)/shard_map/convert.5
  174.7 0.8 fusion.83
  175.8 0.6 fusion.82
  176.5 8.2 %fusion.81 = (bf16[1024,512]{1,0:T(8,128)(2,1)S(1)}, bf16[1024,512]{1,0:T(8,128)(2,1)S(1)}, bf16[1024,512]{1,0:T(8,128)(2,1)S(1)}) fusion(f32[512]{0:T(512)S(1)} %add_convert_fusion.4, f32[1024]{0:T(1024)S(1)} %bitcast_multiply_fusion.4), kind=kLoop, calls=%fused_computation.13.clone.1 | loop fusion | flops 2621440 | bytes 3151872 | tf_op jit(solution)/shard_map/convert.5
  184.7 0.8 fusion.83
  185.6 0.8 all_to_all.30
  186.4 7.4 %all-to-all-start = ((f32[1,16,2048]{2,0,1:T(1,128)}), f32[1,16,2048]{2,0,1:T(1,128)S(1)}, u32[]{:S(2)}, u32[]{:S(2)}) async-start(f32[1,16,2048]{2,0,1:T(1,128)} %all_to_all.30), calls=%async_computation | async-start | bytes 262144 | tf_op jit(solution)/shard_map/all_to_all | solution.py:95
  193.8 7.9 %all-to-all-done = f32[1,16,2048]{2,0,1:T(1,128)S(1)} async-done(((f32[1,16,2048]{2,0,1:T(1,128)}), f32[1,16,2048]{2,0,1:T(1,128)S(1)}, u32[]{:S(2)}, u32[]{:S(2)}) %all-to-all-start) | async-done | bytes 131104 | tf_op jit(solution)/shard_map/all_to_all | solution.py:95
  201.7 0.1 reduce_window_sum.13
  201.9 0.8 copy.13
  202.7 3.5 %all-to-all-start.1 = ((f32[16,1,2048]{2,1,0:T(1,128)}), f32[16,1,2048]{2,1,0:T(1,128)S(1)}, u32[]{:S(2)}, u32[]{:S(2)}) async-start(f32[16,1,2048]{2,1,0:T(1,128)} %copy.13), calls=%async_computation.1 | async-start | bytes 262144 | tf_op jit(solution)/shard_map/all_to_all | solution.py:103
  206.2 0.1 bitcast_divide_fusion
  206.3 0.8 copy.14
  207.1 7.0 %all-to-all-done.1 = f32[16,1,2048]{2,1,0:T(1,128)S(1)} async-done(((f32[16,1,2048]{2,1,0:T(1,128)}), f32[16,1,2048]{2,1,0:T(1,128)S(1)}, u32[]{:S(2)}, u32[]{:S(2)}) %all-to-all-start.1) | async-done | bytes 131104 | tf_op jit(solution)/shard_map/all_to_all | solution.py:103
  214.1 3.5 %all-to-all-start.2 = ((f32[16,1,2048]{2,1,0:T(1,128)}), f32[16,1,2048]{2,1,0:T(1,128)S(1)}, u32[]{:S(2)}, u32[]{:S(2)}) async-start(f32[16,1,2048]{2,1,0:T(1,128)} %copy.14), calls=%async_computation.2 | async-start | bytes 262144 | tf_op jit(solution)/shard_map/all_to_all | solution.py:104
  217.6 0.3 reduce
  217.9 0.7 reshape.260
  218.6 6.9 %all-to-all-done.2 = f32[16,1,2048]{2,1,0:T(1,128)S(1)} async-done(((f32[16,1,2048]{2,1,0:T(1,128)}), f32[16,1,2048]{2,1,0:T(1,128)S(1)}, u32[]{:S(2)}, u32[]{:S(2)}) %all-to-all-start.2) | async-done | bytes 131104 | tf_op jit(solution)/shard_map/all_to_all | solution.py:104
  225.5 0.3 reduce.1
  225.8 0.7 reshape.261
  (109 shorter events, 2.8 us)
Async XLA Ops:
  0.7 56.8 %copy-start.2 = (s32[1,80]{1,0:T(1,128)S(1)}, s32[1,80]{1,0:T(1,128)}, u32[]{:S(2)}) copy-start(s32[1,80]{1,0:T(1,128)} %param.7) | copy-start | bytes 964
  78.4 3.1 %copy-start = (bf16[80,1,128]{1,0,2:T(8,128)(2,1)S(1)}, bf16[80,1,128]{1,0,2:T(8,128)(2,1)}, u32[]{:S(2)}) copy-start(bf16[80,1,128]{1,0,2:T(8,128)(2,1)} %get-tuple-element.244) | copy-start | bytes 61444
  78.4 6.0 %copy-start.1 = (f32[1,3,80]{2,0,1:T(1,128)S(1)}, f32[1,3,80]{2,0,1:T(1,128)}, u32[]{:S(2)}) copy-start(f32[1,3,80]{2,0,1:T(1,128)} %param.8) | copy-start | bytes 2884
  186.4 15.3 %all-to-all-start = ((f32[1,16,2048]{2,0,1:T(1,128)}), f32[1,16,2048]{2,0,1:T(1,128)S(1)}, u32[]{:S(2)}, u32[]{:S(2)}) async-start(f32[1,16,2048]{2,0,1:T(1,128)} %all_to_all.30), calls=%async_computation | async-start | bytes 262144 | tf_op jit(solution)/shard_map/all_to_all | solution.py:95
  202.7 11.4 %all-to-all-start.1 = ((f32[16,1,2048]{2,1,0:T(1,128)}), f32[16,1,2048]{2,1,0:T(1,128)S(1)}, u32[]{:S(2)}, u32[]{:S(2)}) async-start(f32[16,1,2048]{2,1,0:T(1,128)} %copy.13), calls=%async_computation.1 | async-start | bytes 262144 | tf_op jit(solution)/shard_map/all_to_all | solution.py:103
  214.1 11.4 %all-to-all-start.2 = ((f32[16,1,2048]{2,1,0:T(1,128)}), f32[16,1,2048]{2,1,0:T(1,128)S(1)}, u32[]{:S(2)}, u32[]{:S(2)}) async-start(f32[16,1,2048]{2,1,0:T(1,128)} %copy.14), calls=%async_computation.2 | async-start | bytes 262144 | tf_op jit(solution)/shard_map/all_to_all | solution.py:104
where the time goes:
time: 228 us; the launch traced here: 226 us
  other arithmetic  89.6 us (39%)
  local copies, waits for them, and re-layouts  88.7 us (39%)
  waiting for transfers between devices  21.8 us (10%)
  starting transfers between devices  14.4 us (6%)
  matrix products  9.69 us (4%)
    another operation x20, other arithmetic  87.8 us
    unnamed x8, local copies, waits for them, and re-layouts  56.8 us
    gather x1, local copies, waits for them, and re-layouts, spectrum_of(): lax.dynamic_slice_in_dim(one_row, offset, width, 1)  17.8 us
    dot_general x10, matrix products, block_product(): return jnp.dot(left, right, preferred_element_type=jnp.float32)  7.96 us
    all_to_all x1, waiting for transfers between devices, shards(): lax.all_to_all(flattened, 'sub', split_axis=1, concat_axis=0, tiled=True)  7.89 us
    all_to_all x1, starting transfers between devices, shards(): lax.all_to_all(flattened, 'sub', split_axis=1, concat_axis=0, tiled=True)  7.4 us
    all_to_all x1, waiting for transfers between devices, shards(): lax.all_to_all(frame_rows, 'sub', split_axis=0, concat_axis=1, tiled=True)  7 us
    all_to_all x1, waiting for transfers between devices, shards(): lax.all_to_all(cumulative_rows, 'sub', split_axis=0, concat_axis=1, tiled...  6.86 us
  transfers between devices with their start and end apart: 3, of which 3 were waited for; matrix products, arithmetic and copies ran while one was open for 1% of the time, Pallas kernels for 0%

commit v1 on v0

--- a/solution.py
+++ b/solution.py
@@ -100,7 +100,15 @@
     magnitude_factor = jnp.sqrt(jnp.arange(1, members + 1, dtype=jnp.int32).astype(jnp.float32))
     cumulative_rows = running / magnitude_factor[:, None]
     frames_back, cumulative_back = (
-        lax.all_to_all(frame_rows, "sub", split_axis=0, concat_axis=1, tiled=True),
+        jnp.concatenate(
+            lax.all_to_all(
+                jnp.stack(jnp.split(frame_rows, lax.axis_size("sub"), 0), 0),
+                axis_name="sub",
+                split_axis=0,
+                concat_axis=0,
+            ),
+            1,
+        ),
         lax.all_to_all(cumulative_rows, "sub", split_axis=0, concat_axis=1, tiled=True),
     )
     frames = frames_back.reshape(1, 2, rows, cols)

time: 228 us -> 237 us (1.039)
  local copies, waits for them, and re-layouts: 88.7 us -> 97.6 us
    unnamed x8 -> x23, local copies, waits for them, and re-layouts: 56.8 us -> 65.9 us
where the time goes in v1:
time: 237 us; the launch traced here: 235 us
  local copies, waits for them, and re-layouts  97.6 us (41%)
  other arithmetic  89.6 us (38%)
  waiting for transfers between devices  21.8 us (9%)
  starting transfers between devices  14.4 us (6%)
  matrix products  9.69 us (4%)
    another operation x20, other arithmetic  87.8 us
    unnamed x23, local copies, waits for them, and re-layouts  65.9 us
    gather x1, local copies, waits for them, and re-layouts, spectrum_of(): lax.dynamic_slice_in_dim(one_row, offset, width, 1)  17.8 us
    dot_general x10, matrix products, block_product(): return jnp.dot(left, right, preferred_element_type=jnp.float32)  7.96 us
    all_to_all x1, waiting for transfers between devices, shards(): lax.all_to_all(flattened, 'sub', split_axis=1, concat_axis=0, tiled=True)  7.89 us
    all_to_all x1, starting transfers between devices, shards(): lax.all_to_all(flattened, 'sub', split_axis=1, concat_axis=0, tiled=True)  7.4 us
    all_to_all x1, waiting for transfers between devices, shards(): lax.all_to_all(jnp.stack(jnp.split(frame_rows, lax.axis_size('sub'), 0),...  7 us
    all_to_all x1, waiting for transfers between devices, shards(): lax.all_to_all(cumulative_rows, 'sub', split_axis=0, concat_axis=1, tiled...  6.86 us
  transfers between devices with their start and end apart: 3, of which 3 were waited for; matrix products, arithmetic and copies ran while one was open for 1% of the time, Pallas kernels for 0%

profile of v1, /device:TPU:0, one launch (start us, length us, event | category | flops | bytes accessed | tf_op | source)
XLA Modules:
  0.0 235.4 jit_solution(14946589354488242102)
XLA Ops:
  0.7 56.8 %copy.10 = bf16[1,80,2,4096]{2,1,3,0:T(8,128)(2,1)} copy(bf16[1,80,2,4096]{3,2,1,0:T(2,128)(2,1)} %param.6) | data formatting | bytes 2621440 | tf_op args[0]
  57.5 17.8 %gather_fusion = bf16[80,2,128]{1,0,2:T(8,128)(2,1)S(1)} fusion(bf16[80,2,4096]{1,0,2:T(8,128)(2,1)} %bitcast.1, s32[80]{0:T(128)S(1)} %fusion.56), kind=kCustom, calls=%fused_computation | custom fusion | bytes 82880 | tf_op jit(solution)/shard_map/vmap()/gather | solution.py:14
  75.3 3.2 %fusion.73 = (bf16[80,1,128]{1,0,2:T(8,128)(2,1)}, bf16[80,1,128]{1,0,2:T(8,128)(2,1)}) fusion(bf16[80,2,128]{1,0,2:T(8,128)(2,1)S(1)} %gather_fusion), kind=kLoop, calls=%fused_computation.133 | loop fusion | bytes 81920 | tf_op jit(solution)/shard_map/slice | solution.py:24
  78.4 3.1 %copy.11 = bf16[80,1,128]{2,0,1:T(8,128)(2,1)S(1)} copy(bf16[80,1,128]{1,0,2:T(8,128)(2,1)} %get-tuple-element.243) | data formatting | bytes 40960 | tf_op jit(solution)/shard_map/slice | solution.py:24
  81.5 1.6 copy.12
  84.0 0.4 fusion.30
  85.1 0.4 add_multiply_fusion.1
  85.5 100.0 %while.17 = (s32[]{:T(128)}, f32[32,1024]{1,0:T(8,128)S(1)}, f32[80,128]{1,0:T(8,128)S(1)}, f32[80]{0:T(128)S(1)}, f32[80,128]{1,0:T(8,128)S(1)}, /*index=5*/f32...) while((s32[]{:T(128)}, f32[32,1024]{1,0:T(8,128)S(1)}, ...), condition=%wide.region_1.2_spmd.clone.clone, body=%wide.region_0.1_spmd.clone.clone.sunk | while | flops 154242752 | bytes 6879337 | solution.py:92
  85.9 0.6 fusion.82
  86.7 8.2 %fusion.81 = (bf16[1024,512]{1,0:T(8,128)(2,1)S(1)}, bf16[1024,512]{1,0:T(8,128)(2,1)S(1)}, bf16[1024,512]{1,0:T(8,128)(2,1)S(1)}) fusion(f32[512]{0:T(512)S(1)} %add_convert_fusion.4, f32[1024]{0:T(1024)S(1)} %bitcast_multiply_fusion.4), kind=kLoop, calls=%fused_computation.13.clone.1 | loop fusion | flops 2621440 | bytes 3151872 | tf_op jit(solution)/shard_map/convert.5
  94.9 0.8 fusion.83
  95.9 0.6 fusion.82
  96.6 8.2 %fusion.81 = (bf16[1024,512]{1,0:T(8,128)(2,1)S(1)}, bf16[1024,512]{1,0:T(8,128)(2,1)S(1)}, bf16[1024,512]{1,0:T(8,128)(2,1)S(1)}) fusion(f32[512]{0:T(512)S(1)} %add_convert_fusion.4, f32[1024]{0:T(1024)S(1)} %bitcast_multiply_fusion.4), kind=kLoop, calls=%fused_computation.13.clone.1 | loop fusion | flops 2621440 | bytes 3151872 | tf_op jit(solution)/shard_map/convert.5
  104.9 0.8 fusion.83
  105.9 0.6 fusion.82
  106.6 8.2 %fusion.81 = (bf16[1024,512]{1,0:T(8,128)(2,1)S(1)}, bf16[1024,512]{1,0:T(8,128)(2,1)S(1)}, bf16[1024,512]{1,0:T(8,128)(2,1)S(1)}) fusion(f32[512]{0:T(512)S(1)} %add_convert_fusion.4, f32[1024]{0:T(1024)S(1)} %bitcast_multiply_fusion.4), kind=kLoop, calls=%fused_computation.13.clone.1 | loop fusion | flops 2621440 | bytes 3151872 | tf_op jit(solution)/shard_map/convert.5
  114.9 0.8 fusion.83
  115.9 0.6 fusion.82
  116.6 8.2 %fusion.81 = (bf16[1024,512]{1,0:T(8,128)(2,1)S(1)}, bf16[1024,512]{1,0:T(8,128)(2,1)S(1)}, bf16[1024,512]{1,0:T(8,128)(2,1)S(1)}) fusion(f32[512]{0:T(512)S(1)} %add_convert_fusion.4, f32[1024]{0:T(1024)S(1)} %bitcast_multiply_fusion.4), kind=kLoop, calls=%fused_computation.13.clone.1 | loop fusion | flops 2621440 | bytes 3151872 | tf_op jit(solution)/shard_map/convert.5
  124.8 0.8 fusion.83
  125.9 0.6 fusion.82
  126.6 8.2 %fusion.81 = (bf16[1024,512]{1,0:T(8,128)(2,1)S(1)}, bf16[1024,512]{1,0:T(8,128)(2,1)S(1)}, bf16[1024,512]{1,0:T(8,128)(2,1)S(1)}) fusion(f32[512]{0:T(512)S(1)} %add_convert_fusion.4, f32[1024]{0:T(1024)S(1)} %bitcast_multiply_fusion.4), kind=kLoop, calls=%fused_computation.13.clone.1 | loop fusion | flops 2621440 | bytes 3151872 | tf_op jit(solution)/shard_map/convert.5
  134.8 0.8 fusion.83
  135.8 0.6 fusion.82
  136.6 8.2 %fusion.81 = (bf16[1024,512]{1,0:T(8,128)(2,1)S(1)}, bf16[1024,512]{1,0:T(8,128)(2,1)S(1)}, bf16[1024,512]{1,0:T(8,128)(2,1)S(1)}) fusion(f32[512]{0:T(512)S(1)} %add_convert_fusion.4, f32[1024]{0:T(1024)S(1)} %bitcast_multiply_fusion.4), kind=kLoop, calls=%fused_computation.13.clone.1 | loop fusion | flops 2621440 | bytes 3151872 | tf_op jit(solution)/shard_map/convert.5
  144.8 0.8 fusion.83
  145.8 0.6 fusion.82
  146.5 8.2 %fusion.81 = (bf16[1024,512]{1,0:T(8,128)(2,1)S(1)}, bf16[1024,512]{1,0:T(8,128)(2,1)S(1)}, bf16[1024,512]{1,0:T(8,128)(2,1)S(1)}) fusion(f32[512]{0:T(512)S(1)} %add_convert_fusion.4, f32[1024]{0:T(1024)S(1)} %bitcast_multiply_fusion.4), kind=kLoop, calls=%fused_computation.13.clone.1 | loop fusion | flops 2621440 | bytes 3151872 | tf_op jit(solution)/shard_map/convert.5
  154.8 0.8 fusion.83
  155.8 0.6 fusion.82
  156.5 8.2 %fusion.81 = (bf16[1024,512]{1,0:T(8,128)(2,1)S(1)}, bf16[1024,512]{1,0:T(8,128)(2,1)S(1)}, bf16[1024,512]{1,0:T(8,128)(2,1)S(1)}) fusion(f32[512]{0:T(512)S(1)} %add_convert_fusion.4, f32[1024]{0:T(1024)S(1)} %bitcast_multiply_fusion.4), kind=kLoop, calls=%fused_computation.13.clone.1 | loop fusion | flops 2621440 | bytes 3151872 | tf_op jit(solution)/shard_map/convert.5
  164.8 0.8 fusion.83
  165.8 0.6 fusion.82
  166.5 8.2 %fusion.81 = (bf16[1024,512]{1,0:T(8,128)(2,1)S(1)}, bf16[1024,512]{1,0:T(8,128)(2,1)S(1)}, bf16[1024,512]{1,0:T(8,128)(2,1)S(1)}) fusion(f32[512]{0:T(512)S(1)} %add_convert_fusion.4, f32[1024]{0:T(1024)S(1)} %bitcast_multiply_fusion.4), kind=kLoop, calls=%fused_computation.13.clone.1 | loop fusion | flops 2621440 | bytes 3151872 | tf_op jit(solution)/shard_map/convert.5
  174.7 0.8 fusion.83
  175.8 0.6 fusion.82
  176.5 8.2 %fusion.81 = (bf16[1024,512]{1,0:T(8,128)(2,1)S(1)}, bf16[1024,512]{1,0:T(8,128)(2,1)S(1)}, bf16[1024,512]{1,0:T(8,128)(2,1)S(1)}) fusion(f32[512]{0:T(512)S(1)} %add_convert_fusion.4, f32[1024]{0:T(1024)S(1)} %bitcast_multiply_fusion.4), kind=kLoop, calls=%fused_computation.13.clone.1 | loop fusion | flops 2621440 | bytes 3151872 | tf_op jit(solution)/shard_map/convert.5
  184.7 0.8 fusion.83
  185.6 0.8 all_to_all.23
  186.4 7.4 %all-to-all-start = ((f32[1,16,2048]{2,0,1:T(1,128)}), f32[1,16,2048]{2,0,1:T(1,128)S(1)}, u32[]{:S(2)}, u32[]{:S(2)}) async-start(f32[1,16,2048]{2,0,1:T(1,128)} %all_to_all.23), calls=%async_computation | async-start | bytes 262144 | tf_op jit(solution)/shard_map/all_to_all | solution.py:95
  193.8 7.9 %all-to-all-done = f32[1,16,2048]{2,0,1:T(1,128)S(1)} async-done(((f32[1,16,2048]{2,0,1:T(1,128)}), f32[1,16,2048]{2,0,1:T(1,128)S(1)}, u32[]{:S(2)}, u32[]{:S(2)}) %all-to-all-start) | async-done | bytes 131104 | tf_op jit(solution)/shard_map/all_to_all | solution.py:95
  201.9 0.6 constant_dynamic-update-slice_fusion.15
  202.5 0.6 constant_dynamic-update-slice_fusion.14
  203.1 0.6 constant_dynamic-update-slice_fusion.13
  203.7 0.6 constant_dynamic-update-slice_fusion.12
  204.3 0.6 constant_dynamic-update-slice_fusion.11
  204.9 0.6 constant_dynamic-update-slice_fusion.10
  205.5 0.6 constant_dynamic-update-slice_fusion.9
  206.1 0.6 constant_dynamic-update-slice_fusion.8
  206.7 0.6 constant_dynamic-update-slice_fusion.7
  207.3 0.6 constant_dynamic-update-slice_fusion.6
  207.9 0.6 constant_dynamic-update-slice_fusion.5
  208.5 0.6 constant_dynamic-update-slice_fusion.4
  209.2 0.6 constant_dynamic-update-slice_fusion.3
  209.8 0.6 constant_dynamic-update-slice_fusion.2
  210.4 0.6 constant_dynamic-update-slice_fusion.1
  211.0 0.6 constant_dynamic-update-slice_fusion
  211.6 3.5 %all-to-all-start.1 = ((f32[16,1,2048]{2,1,0:T(1,128)}), f32[16,1,2048]{2,1,0:T(1,128)S(1)}, u32[]{:S(2)}, u32[]{:S(2)}) async-start(f32[16,1,2048]{2,1,0:T(1,128)} %constant_dynamic-update-slice_fusion), calls=%async_computation.1 | async-start | bytes 262144 | tf_op jit(solution)/shard_map/all_to_all | solution.py:104
  215.2 0.8 copy.13
  216.0 7.0 %all-to-all-done.1 = f32[16,1,2048]{2,1,0:T(1,128)S(1)} async-done(((f32[16,1,2048]{2,1,0:T(1,128)}), f32[16,1,2048]{2,1,0:T(1,128)S(1)}, u32[]{:S(2)}, u32[]{:S(2)}) %all-to-all-start.1) | async-done | bytes 131104 | tf_op jit(solution)/shard_map/all_to_all | solution.py:104
  223.0 3.5 %all-to-all-start.2 = ((f32[16,1,2048]{2,1,0:T(1,128)}), f32[16,1,2048]{2,1,0:T(1,128)S(1)}, u32[]{:S(2)}, u32[]{:S(2)}) async-start(f32[16,1,2048]{2,1,0:T(1,128)} %copy.13), calls=%async_computation.2 | async-start | bytes 262144 | tf_op jit(solution)/shard_map/all_to_all | solution.py:112
  226.8 0.7 reshape_reshape.3
  227.5 6.9 %all-to-all-done.2 = f32[16,1,2048]{2,1,0:T(1,128)S(1)} async-done(((f32[16,1,2048]{2,1,0:T(1,128)}), f32[16,1,2048]{2,1,0:T(1,128)S(1)}, u32[]{:S(2)}, u32[]{:S(2)}) %all-to-all-start.2) | async-done | bytes 131104 | tf_op jit(solution)/shard_map/all_to_all | solution.py:112
  234.7 0.7 reshape.250
  (124 shorter events, 5.2 us)
Async XLA Ops:
  0.7 56.8 %copy-start.2 = (s32[1,80]{1,0:T(1,128)S(1)}, s32[1,80]{1,0:T(1,128)}, u32[]{:S(2)}) copy-start(s32[1,80]{1,0:T(1,128)} %param.7) | copy-start | bytes 964
  78.4 3.1 %copy-start = (bf16[80,1,128]{1,0,2:T(8,128)(2,1)S(1)}, bf16[80,1,128]{1,0,2:T(8,128)(2,1)}, u32[]{:S(2)}) copy-start(bf16[80,1,128]{1,0,2:T(8,128)(2,1)} %get-tuple-element.244) | copy-start | bytes 61444
  78.4 6.0 %copy-start.1 = (f32[1,3,80]{2,0,1:T(1,128)S(1)}, f32[1,3,80]{2,0,1:T(1,128)}, u32[]{:S(2)}) copy-start(f32[1,3,80]{2,0,1:T(1,128)} %param.8) | copy-start | bytes 2884
  186.4 15.3 %all-to-all-start = ((f32[1,16,2048]{2,0,1:T(1,128)}), f32[1,16,2048]{2,0,1:T(1,128)S(1)}, u32[]{:S(2)}, u32[]{:S(2)}) async-start(f32[1,16,2048]{2,0,1:T(1,128)} %all_to_all.23), calls=%async_computation | async-start | bytes 262144 | tf_op jit(solution)/shard_map/all_to_all | solution.py:95
  211.6 11.4 %all-to-all-start.1 = ((f32[16,1,2048]{2,1,0:T(1,128)}), f32[16,1,2048]{2,1,0:T(1,128)S(1)}, u32[]{:S(2)}, u32[]{:S(2)}) async-start(f32[16,1,2048]{2,1,0:T(1,128)} %constant_dynamic-update-slice_fusion), calls=%async_computation.1 | async-start | bytes 262144 | tf_op jit(solution)/shard_map/all_to_all | solution.py:104
  223.0 11.4 %all-to-all-start.2 = ((f32[16,1,2048]{2,1,0:T(1,128)}), f32[16,1,2048]{2,1,0:T(1,128)S(1)}, u32[]{:S(2)}, u32[]{:S(2)}) async-start(f32[16,1,2048]{2,1,0:T(1,128)} %copy.13), calls=%async_computation.2 | async-start | bytes 262144 | tf_op jit(solution)/shard_map/all_to_all | solution.py:112
